TPU v7x, 512 devices: a whole 4x4x16 slice. The times are simulated.
512 devices in a mesh: ctx: 32 (over z, core), ch: 16 (over x, y).
Axes of the slice: x: 4, y: 4, z: 16, core: 2. Of those that a mesh axis runs over, the one named last changes fastest.
Arguments:
- query_in: bfloat16 [8192, 4096], P('ctx', 'ch'), may hold values from -63 to 63
- key_in: bfloat16 [8192, 4096], P('ctx', 'ch'), may hold values from -4 to 4
- value_in: bfloat16 [8192, 4096], P('ctx', 'ch'), may hold values from -4 to 4
- short_taps: float32 [7, 3, 4096], P(None, None, 'ch'), may hold values from -2 to 2
- residues: float32 [4096, 16], P('ch'), may hold values from -1.5 to 1.5
- decays: float32 [4096, 16], P('ch'), may hold values from 6.1035157e-06 to 0.02
- out_weight: bfloat16 [4096, 4096], P('ch'), may hold values from -0.125 to 0.125
- out_grad: bfloat16 [8192, 4096], P('ctx', 'ch'), may hold values from -6 to 6
Outputs:
- projected: bfloat16 [8192, 4096], P('ctx', 'ch')
- grad_query: bfloat16 [8192, 4096], P('ctx', 'ch')
- grad_key: bfloat16 [8192, 4096], P('ctx', 'ch')
- grad_value: bfloat16 [8192, 4096], P('ctx', 'ch')
All inputs are finite; a program needn't handle non-finite values.
Results may differ from a plain program's by a relative error of at most 0.0058.
Values may be sent and summed in bfloat16 or wider, within the bound.
A program may use at most 64 MiB of HBM per device.

v0:
```python
import jax
import jax.numpy as jnp
import numpy as np
from jax import lax
from jax.sharding import PartitionSpec as P

block_len = 64
exact_precision = lax.Precision.HIGHEST


def from_behind(value, axis, steps):
    count = lax.axis_size(axis)
    leading, last = (max(0, -steps), min(count, count - steps))
    return lax.ppermute(value, axis, [(source, source + steps) for source in range(leading, last)])


def one_hot_table():
    indices = np.arange(block_len)
    return (indices[None, :, None] - indices[None, None, :] == indices[:, None, None]).astype(
        np.float32
    )


def modal_tables(residues, decays):
    offsets = jnp.arange(block_len, dtype=jnp.float32)
    scaled = residues * jnp.sqrt(decays)
    filter_head = jnp.einsum(
        "cn,cnd->cd", scaled, jnp.exp(-decays[:, :, None] * offsets), precision=exact_precision
    )
    toeplitz = jnp.einsum(
        "cd,dij->cij", filter_head, jnp.asarray(one_hot_table()), precision=exact_precision
    )
    decay_in = jnp.exp(-decays[:, :, None] * (block_len - 1.0 - offsets))
    decay_out = scaled[:, :, None] * jnp.exp(-decays[:, :, None] * (offsets + 1.0))
    return (toeplitz, decay_in, decay_out)


def combine(earlier, latter):
    return (earlier[0] * latter[1] + latter[0], earlier[1] * latter[1])


def prepare(signal, decays, decay_tables):
    channels, length = signal.shape
    pieces = length // block_len
    block_list = signal.reshape(channels, pieces, block_len)
    within_block = jnp.einsum(
        "cij,cbj->cbi", decay_tables[0], block_list, precision=exact_precision
    )
    block_final_states = jnp.einsum(
        "avp,axp->avx", block_list, decay_tables[1], precision=exact_precision
    )
    factor = jnp.broadcast_to(jnp.exp(-decays * block_len)[:, None, :], block_final_states.shape)
    running, _ = lax.associative_scan(combine, (block_final_states, factor), axis=1)
    return (within_block, running)


def finish(within_block, running, decays, incoming, decay_tables):
    channels, pieces, _ = within_block.shape
    earlier_sum = jnp.concatenate([jnp.zeros_like(running[:, :1]), running[:, :-1]], axis=1)
    starts = jnp.arange(pieces, dtype=jnp.float32) * block_len
    carried_state = (
        earlier_sum + jnp.exp(-decays[:, None, :] * starts[None, :, None]) * incoming[:, None, :]
    )
    final_output = within_block + jnp.einsum(
        "lpe,leo->lpo", carried_state, decay_tables[2], precision=exact_precision
    )
    return final_output.reshape(channels, pieces * block_len)


def channel_params(residues, decays):
    part_size = residues.shape[0] // lax.axis_size("ctx")
    first_chan = lax.axis_index("ctx") * part_size
    residues = lax.dynamic_slice_in_dim(residues, first_chan, part_size, 0)
    decays = lax.dynamic_slice_in_dim(decays, first_chan, part_size, 0)
    return (decays, modal_tables(residues, decays))


def long_forward(mixed_values, decays, decay_tables):
    sequence = lax.all_to_all(mixed_values.T, "ctx", split_axis=0, concat_axis=1, tiled=True)
    within_block, running = prepare(sequence.astype(jnp.float32), decays, decay_tables)
    final_output = finish(
        within_block, running, decays, jnp.zeros(decays.shape, jnp.float32), decay_tables
    )
    return lax.all_to_all(final_output, "ctx", split_axis=1, concat_axis=0, tiled=True).T


def long_backward(grad_mixed, decays, decay_tables):
    sequence = lax.all_to_all(grad_mixed.T, "ctx", split_axis=0, concat_axis=1, tiled=True)
    within_block, running = prepare(jnp.flip(sequence.astype(jnp.float32), 1), decays, decay_tables)
    final_output = jnp.flip(
        finish(within_block, running, decays, jnp.zeros(decays.shape, jnp.float32), decay_tables), 1
    )
    return lax.all_to_all(final_output, "ctx", split_axis=1, concat_axis=0, tiled=True).T


def shards(query_in, key_in, value_in, short_taps, residues, decays, out_weight, out_grad):
    length = query_in.shape[0]
    rim_len = short_taps.shape[0] - 1
    stacked = jnp.stack([query_in, key_in, value_in])
    ahead_rows = from_behind(stacked[:, length - rim_len :], "ctx", 1)
    extended = jnp.concatenate([ahead_rows, stacked], axis=1).astype(jnp.float32)
    featured = jnp.zeros(stacked.shape, jnp.float32)
    for tap_index in range(rim_len + 1):
        begin = rim_len - tap_index
        featured = (
            featured + short_taps[tap_index][:, None, :] * extended[:, begin : begin + length]
        )
    query_feat = featured[0]
    key_feat = featured[1]
    value_feat = featured[2]
    mixed_values = (key_feat * value_feat).astype(jnp.bfloat16)
    used_decays, decay_tables = channel_params(residues, decays)
    conv_out = long_forward(mixed_values, used_decays, decay_tables)
    gated = (query_feat * conv_out).astype(jnp.bfloat16)
    partial_proj = jnp.dot(gated, out_weight, preferred_element_type=jnp.float32)
    projected = lax.psum_scatter(partial_proj, "ch", scatter_dimension=1, tiled=True).astype(
        jnp.bfloat16
    )
    grad_gated = jnp.einsum(
        "te,ce->tc",
        lax.all_gather(out_grad, "ch", axis=1, tiled=True),
        out_weight,
        preferred_element_type=jnp.float32,
    )
    grad_query_feat = (grad_gated * conv_out).astype(jnp.bfloat16)
    grad_mixed = (grad_gated * query_feat).astype(jnp.bfloat16)
    grad_conv = long_backward(grad_mixed, used_decays, decay_tables)
    grad_key_feat = (grad_conv * value_feat).astype(jnp.bfloat16)
    grad_value_feat = (grad_conv * key_feat).astype(jnp.bfloat16)
    grad_feats = jnp.stack([grad_query_feat, grad_key_feat, grad_value_feat])
    behind = from_behind(grad_feats[:, :rim_len], "ctx", -1)
    widened = jnp.concatenate([grad_feats, behind], axis=1).astype(jnp.float32)
    grad_stack = jnp.zeros(grad_feats.shape, jnp.float32)
    for tap_index in range(rim_len + 1):
        grad_stack = (
            grad_stack
            + short_taps[tap_index][:, None, :] * widened[:, tap_index : tap_index + length]
        )
    grad_stack = grad_stack.astype(jnp.bfloat16)
    return (projected, grad_stack[0], grad_stack[1], grad_stack[2])


def solution(mesh):
    in_specs = (
        P("ctx", "ch"),
        P("ctx", "ch"),
        P("ctx", "ch"),
        P(None, None, "ch"),
        P("ch", None),
        P("ch", None),
        P("ch", None),
        P("ctx", "ch"),
    )
    out_specs = (P("ctx", "ch"), P("ctx", "ch"), P("ctx", "ch"), P("ctx", "ch"))
    return jax.shard_map(shards, mesh=mesh, in_specs=in_specs, out_specs=out_specs, check_vma=False)
```

profile of v0, /device:TPU:32, one launch (start us, length us, event | category | flops | bytes accessed | tf_op | source)
XLA Modules:
  0.0 459.0 jit_solution(5360661742519281431)
XLA Ops:
  8.6 1.9 collective-permute-start
  18.3 59.2 %all-gather.2.cloned.1.call-done = bf16[256,4096]{1,0:T(8,128)(2,1)} async-done(((bf16[256,256]{1,0:T(8,128)(2,1)}), bf16[256,4096]{1,0:T(8,128)(2,1)}) %all-gather.2.cloned.1.call-update) | async-done | bytes 2097168 | tf_op jit(solution)/shard_map/all_gather | solution.py:121
  77.4 2.3 fusion.74
  80.6 12.8 %all-to-all-start.2 = ((bf16[32,8,256]{2,1,0:T(8,128)(2,1)}), bf16[32,8,256]{2,1,0:T(8,128)(2,1)S(1)}, u32[]{:S(2)}, u32[]{:S(2)}) async-start(bf16[32,8,256]{2,1,0:T(8,128)(2,1)} %bitcast.21), calls=%async_computation.3 | async-start | bytes 262144 | tf_op jit(solution)/shard_map/all_to_all | solution.py:88
  93.9 3.4 fusion.73
  97.3 11.8 %all-to-all-done.2 = bf16[32,8,256]{2,1,0:T(8,128)(2,1)S(1)} async-done(((bf16[32,8,256]{2,1,0:T(8,128)(2,1)}), bf16[32,8,256]{2,1,0:T(8,128)(2,1)S(1)}, u32[]{:S(2)}, u32[]{:S(2)}) %all-to-all-start.2) | async-done | bytes 131104 | tf_op jit(solution)/shard_map/all_to_all | solution.py:88
  109.1 21.2 %rev.7 = f32[8,8192]{1,0:T(8,128)} reverse(f32[8,8192]{1,0:T(8,128)S(1)} %bitcast.137), dimensions={1} | reverse | bytes 524288 | tf_op jit(solution)/shard_map/jit(_flip)/rev | solution.py:89
  131.5 1.6 fusion.42
  133.0 1.8 slice.453
  136.0 1.8 slice.423
  146.2 1.6 multiply_add_fusion.3
  147.7 1.6 slice.447
  149.4 1.7 slice.433
  151.1 1.7 slice.432
  152.7 1.6 multiply_add_fusion.2
  154.3 1.6 slice.445
  155.9 1.6 slice.436
  157.5 1.6 slice.435
  161.4 2.8 fusion.17
  170.7 3.2 pad.107
  176.2 3.2 pad.109
  186.3 1.6 pad.161
  187.9 1.6 pad.217
  189.5 2.1 convolution_add_fusion
  193.7 24.0 %rev.8 = f32[8,8192]{1,0:T(8,128)S(1)} reverse(f32[8,8192]{1,0:T(8,128)} %reshape.69), dimensions={1} | reverse | bytes 524288 | tf_op jit(solution)/shard_map/jit(_flip)/rev | solution.py:90
  217.7 26.1 %all_to_all.67 = f32[8,32,256]{2,0,1:T(8,128)} all-to-all(f32[8,32,256]{2,0,1:T(8,128)S(1)} %bitcast.138), channel_id=1, replica_groups=mesh['ctx'=32,'ch'=16] {'ctx'}, dimensions={1} | all-to-all | bytes 524288 | tf_op jit(solution)/shard_map/all_to_all | solution.py:93
  246.7 20.7 %all_to_all.68 = bf16[32,8,256]{2,1,0:T(8,128)(2,1)S(1)} all-to-all(bf16[32,8,256]{2,1,0:T(8,128)(2,1)S(1)} %bitcast.147), channel_id=1, replica_groups=mesh['ctx'=32,'ch'=16] {'ctx'}, dimensions={0} | all-to-all | bytes 262144 | tf_op jit(solution)/shard_map/all_to_all | solution.py:79
  269.1 1.3 fusion.19
  271.6 1.8 slice.420
  285.0 1.6 fusion.71
  287.3 3.1 pad.91
  294.3 4.9 %pad.92 = f32[8,8,16]{1,2,0:T(8,128)} pad(f32[8,4,16]{1,2,0:T(8,128)} %pad_maximum_fusion.1, f32[]{:T(128)} %constant.7.clone.1), padding=0_0_0x0_1_1x0_0_0 | pad | bytes 6148 | tf_op jit(solution)/shard_map/pad | solution.py:53
  299.2 4.9 %pad.93 = f32[8,8,16]{1,2,0:T(8,128)} pad(f32[8,4,16]{1,2,0:T(8,128)} %add.260, f32[]{:T(128)} %constant.7.clone.1), padding=0_0_0x1_0_1x0_0_0 | pad | bytes 6148 | tf_op jit(solution)/shard_map/pad | solution.py:53
  304.1 1.5 add.262
  307.3 3.2 pad.94
  310.5 5.0 %pad.95 = f32[8,16,16]{1,2,0:T(8,128)} pad(f32[8,8,16]{1,2,0:T(8,128)} %add.262, f32[]{:T(128)} %constant.7.clone.1), padding=0_0_0x1_0_1x0_0_0 | pad | bytes 12292 | tf_op jit(solution)/shard_map/pad | solution.py:53
  315.5 1.5 add.264
  318.8 3.3 pad.97
  324.8 3.5 pad.99
  329.3 1.6 pad.159
  330.9 1.6 pad.216
  332.6 2.1 convolution_add_fusion.1
  337.8 25.2 %all_to_all.69 = f32[8,32,256]{2,0,1:T(8,128)S(1)} all-to-all(f32[8,32,256]{2,0,1:T(8,128)S(1)} %copy.85), channel_id=1, replica_groups=mesh['ctx'=32,'ch'=16] {'ctx'}, dimensions={1} | all-to-all | bytes 524288 | tf_op jit(solution)/shard_map/all_to_all | solution.py:84
  363.2 2.7 fusion.24
  366.9 2.5 collective-permute-start.1
  369.5 1.4 collective-permute-done.1
  372.4 78.1 %reduce-scatter.2.cloned.1.call-done = f32[256,256]{1,0:T(8,128)} async-done(((f32[256,4096]{1,0:T(8,128)}), f32[256,256]{1,0:T(8,128)}) %reduce-scatter.2.cloned.1.call-update) | async-done | bytes 262160 | tf_op jit(solution)/shard_map/reduce_scatter | solution.py:116
  450.5 1.6 convert_element_type.43
  (187 shorter events, 75.7 us)
Async XLA Ops:
  7.2 70.3 %copy-start = (bf16[256,4096]{1,0:T(8,128)(2,1)S(1)}, bf16[256,4096]{1,0:T(8,128)(2,1)}, u32[]{:S(2)}) copy-start(bf16[256,4096]{1,0:T(8,128)(2,1)} %param.15) | copy-start | bytes 6291460
  7.2 70.2 %all-gather.2.cloned.1.call-start = ((), (), s32[]{:S(2)}) async-start(), calls=%async_computation.6 | async-start | bytes 2228224 | tf_op jit(solution)/shard_map/all_gather | solution.py:121
  8.6 7.8 %collective-permute-start = (bf16[3,6,256]{2,1,0:T(8,128)(2,1)S(1)}, bf16[3,6,256]{2,1,0:T(8,128)(2,1)S(1)}, u32[]{:S(2)}, u32[]{:S(2)}) collective-permute-start(bf16[3,6,256]{2,1,0:T(8,128)(2,1)S(1)} %pad_maximum_fusion.14), channel_id=1, source_target_pairs={{0,16},{16,32},{32,48},{48,64},{64,80},{80,96},{96,112},{112,128},... | collective-permute-start | bytes 27656 | tf_op jit(solution)/shard_map/ppermute | solution.py:14
  13.6 4.6 copy-start.16
  13.6 4.6 copy-start.18
  13.7 4.5 copy-start.20
  13.7 4.5 copy-start.22
  13.7 4.5 copy-start.24
  13.7 4.5 copy-start.26
  14.3 79.3 %copy-start.14 = (f32[8,16]{1,0:T(8,128)}, f32[8,16]{1,0:T(8,128)S(1)}, u32[]{:S(2)}) copy-start(f32[8,16]{1,0:T(8,128)S(1)} %get-tuple-element.34) | copy-start | bytes 1540
  14.9 3.3 copy-start.28
  79.8 29.4 %copy-start.1 = (f32[256,256]{1,0:T(8,128)}, f32[256,256]{1,0:T(8,128)S(1)}, u32[]{:S(2)}) copy-start(f32[256,256]{1,0:T(8,128)S(1)} %fusion.74) | copy-start | bytes 786436
  80.6 28.5 %all-to-all-start.2 = ((bf16[32,8,256]{2,1,0:T(8,128)(2,1)}), bf16[32,8,256]{2,1,0:T(8,128)(2,1)S(1)}, u32[]{:S(2)}, u32[]{:S(2)}) async-start(bf16[32,8,256]{2,1,0:T(8,128)(2,1)} %bitcast.21), calls=%async_computation.3 | async-start | bytes 262144 | tf_op jit(solution)/shard_map/all_to_all | solution.py:88
  93.4 357.1 %reduce-scatter.2.cloned.1.call-start = ((), (), s32[]{:S(2)}) async-start(), calls=%async_computation.5 | async-start | bytes 4456448 | tf_op jit(solution)/shard_map/reduce_scatter | solution.py:116
  133.0 4.7 %copy-start.8 = (f32[8,128,16]{1,2,0:T(8,128)}, f32[8,128,16]{1,2,0:T(8,128)S(1)}, u32[]{:S(2)}) copy-start(f32[8,128,16]{1,2,0:T(8,128)S(1)} %fusion.42) | copy-start | bytes 196612
  143.3 15.8 %copy-start.4 = (f32[8,32,16]{1,2,0:T(8,128)}, f32[8,32,16]{1,2,0:T(8,128)S(1)}, u32[]{:S(2)}) copy-start(f32[8,32,16]{1,2,0:T(8,128)S(1)} %multiply_add_fusion.4) | copy-start | bytes 49156
  164.2 5.8 %copy-start.7 = (f32[8,8,16]{1,2,0:T(8,128)S(1)}, f32[8,8,16]{1,2,0:T(8,128)}, u32[]{:S(2)}) copy-start(f32[8,8,16]{1,2,0:T(8,128)} %multiply_add_fusion.2) | copy-start | bytes 12292
  164.2 11.2 %copy-start.6 = (f32[8,16,16]{1,2,0:T(8,128)S(1)}, f32[8,16,16]{1,2,0:T(8,128)}, u32[]{:S(2)}) copy-start(f32[8,16,16]{1,2,0:T(8,128)} %multiply_add_fusion.3) | copy-start | bytes 24580
  164.2 16.2 %copy-start.5 = (f32[8,32,16]{1,2,0:T(8,128)S(1)}, f32[8,32,16]{1,2,0:T(8,128)}, u32[]{:S(2)}) copy-start(f32[8,32,16]{1,2,0:T(8,128)} %copy-done.4) | copy-start | bytes 49156
  168.4 17.8 %copy-start.9 = (f32[8,128,16]{1,2,0:T(8,128)S(1)}, f32[8,128,16]{1,2,0:T(8,128)}, u32[]{:S(2)}) copy-start(f32[8,128,16]{1,2,0:T(8,128)} %copy-done.8) | copy-start | bytes 196612
  170.1 19.5 %copy-start.12 = (f32[8,128,64]{1,2,0:T(8,128)S(1)}, f32[8,128,64]{1,2,0:T(8,128)}, u32[]{:S(2)}) copy-start(f32[8,128,64]{1,2,0:T(8,128)} %fusion.17) | copy-start | bytes 786436
  193.7 75.4 %copy-start.3 = (f32[8,64,64]{2,0,1:T(8,128)S(1)}, f32[8,64,64]{2,0,1:T(8,128)}, u32[]{:S(2)}) copy-start(f32[8,64,64]{2,0,1:T(8,128)} %fusion.73) | copy-start | bytes 393220
  271.6 9.6 %copy-start.13 = (f32[8,16]{1,0:T(8,128)S(1)}, f32[8,16]{1,0:T(8,128)}, u32[]{:S(2)}) copy-start(f32[8,16]{1,0:T(8,128)} %get-tuple-element.30) | copy-start | bytes 1540
  294.3 38.3 %copy-start.11 = (f32[8,128,64]{1,2,0:T(8,128)S(1)}, f32[8,128,64]{1,2,0:T(8,128)}, u32[]{:S(2)}) copy-start(f32[8,128,64]{1,2,0:T(8,128)} %fusion.19) | copy-start | bytes 786436
  317.9 14.7 %copy-start.15 = (f32[8,16]{1,0:T(8,128)S(1)}, f32[8,16]{1,0:T(8,128)}, u32[]{:S(2)}) copy-start(f32[8,16]{1,0:T(8,128)} %copy-done.14) | copy-start | bytes 1540
  365.9 0.9 copy-start.2
  365.9 1.0 copy-start.10
  366.8 4.1 copy-start.17
  366.8 4.1 copy-start.19
  366.8 4.1 copy-start.21
  366.8 4.1 copy-start.23
  366.8 4.1 copy-start.25
  366.8 4.1 copy-start.27
  366.8 4.1 copy-start.29
  366.9 3.9 collective-permute-start.1
Sparse Core Ops, SparseCore 0:
  11.0 66.3 all-gather.1
  366.0 84.4 reduce-scatter.1
where the time goes:
time: 464 us; the launch traced here: 459 us
  waiting for transfers between devices  151 us (33%)
  local copies, waits for them, and re-layouts  144 us (31%)
  blocking collectives  72 us (16%)
  other arithmetic  40 us (9%)
  matrix products  19.7 us (4%)
  starting transfers between devices  17.5 us (4%)
  between operations  15 us (3%)
    reduce_scatter x1, waiting for transfers between devices, shards(): lax.psum_scatter(partial_proj, 'ch', scatter_dimension=1, tiled=True)  78.1 us
    all_gather x1, waiting for transfers between devices, shards(): lax.all_gather(out_grad, 'ch', axis=1, tiled=True)  59.2 us
    pad x20, local copies, waits for them, and re-layouts, prepare(): lax.associative_scan(combine, (block_final_states, factor), axis=1)  42.8 us
    slice x34, local copies, waits for them, and re-layouts, prepare(): lax.associative_scan(combine, (block_final_states, factor), axis=1)  32.8 us
    all_to_all x1, blocking collectives, long_backward(): lax.all_to_all(final_output, 'ctx', split_axis=1, concat_axis=0, tiled=True)  26.1 us
    all_to_all x1, blocking collectives, long_forward(): lax.all_to_all(final_output, 'ctx', split_axis=1, concat_axis=0, tiled=True)  25.2 us
    rev x1, local copies, waits for them, and re-layouts, long_backward(): jnp.flip(finish(within_block, running, decays, jnp.zeros(decays.shape, jn...  24 us
    rev x1, local copies, waits for them, and re-layouts, long_backward(): jnp.flip(sequence.astype(jnp.float32), 1)  21.2 us
  transfers between devices with their start and end apart: 5, of which 4 were waited for; matrix products, arithmetic and copies ran while one was open for 3% of the time, Pallas kernels for 0%

commit v1 on v0

--- a/solution.py
+++ b/solution.py
@@ -118,7 +118,9 @@
     )
     grad_gated = jnp.einsum(
         "te,ce->tc",
-        lax.all_gather(out_grad, "ch", axis=1, tiled=True),
+        jnp.concatenate(
+            lax.all_to_all(jnp.stack([out_grad] * lax.axis_size("ch")), "ch", 0, 0), axis=1
+        ),
         out_weight,
         preferred_element_type=jnp.float32,
     )

time: 464 us -> 442 us (0.953)
  waiting for transfers between devices: 151 us -> 119 us
  starting transfers between devices: 17.5 us -> 28.1 us
    all_gather x1 -> x0, waiting for transfers between devices: 59.2 us -> none  [shards(): lax.all_gather(out_grad, 'ch', axis=1, tiled=True)]
    all_to_all x0 -> x1, waiting for transfers between devices: none -> 25.9 us  [shards(): lax.all_to_all(jnp.stack([out_grad] * lax.axis_size('ch')), 'ch', 0, 0)]
    all_to_all x0 -> x1, starting transfers between devices: none -> 7.23 us  [shards(): lax.all_to_all(jnp.stack([out_grad] * lax.axis_size('ch')), 'ch', 0, 0)]
where the time goes in v1:
time: 442 us; the launch traced here: 437 us
  local copies, waits for them, and re-layouts  145 us (33%)
  waiting for transfers between devices  119 us (27%)
  blocking collectives  72 us (16%)
  other arithmetic  38.5 us (9%)
  starting transfers between devices  28.1 us (6%)
  matrix products  19.1 us (4%)
  between operations  15.1 us (3%)
    reduce_scatter x1, waiting for transfers between devices, shards(): lax.psum_scatter(partial_proj, 'ch', scatter_dimension=1, tiled=True)  80.3 us
    pad x20, local copies, waits for them, and re-layouts, prepare(): lax.associative_scan(combine, (block_final_states, factor), axis=1)  42.8 us
    slice x34, local copies, waits for them, and re-layouts, prepare(): lax.associative_scan(combine, (block_final_states, factor), axis=1)  32.8 us
    all_to_all x1, blocking collectives, long_backward(): lax.all_to_all(final_output, 'ctx', split_axis=1, concat_axis=0, tiled=True)  26.1 us
    all_to_all x1, waiting for transfers between devices, shards(): lax.all_to_all(jnp.stack([out_grad] * lax.axis_size('ch')), 'ch', 0, 0)  25.9 us
    all_to_all x1, blocking collectives, long_forward(): lax.all_to_all(final_output, 'ctx', split_axis=1, concat_axis=0, tiled=True)  25.2 us
    rev x1, local copies, waits for them, and re-layouts, long_backward(): jnp.flip(finish(within_block, running, decays, jnp.zeros(decays.shape, jn...  23.9 us
    rev x1, local copies, waits for them, and re-layouts, long_backward(): jnp.flip(sequence.astype(jnp.float32), 1)  21.2 us
  transfers between devices with their start and end apart: 5, of which 4 were waited for; matrix products, arithmetic and copies ran while one was open for 3% of the time, Pallas kernels for 0%

profile of v1, /device:TPU:32, one launch (start us, length us, event | category | flops | bytes accessed | tf_op | source)
XLA Modules:
  0.0 437.1 jit_solution(2685100510612163613)
XLA Ops:
  8.1 1.9 collective-permute-start
  11.0 1.6 stack.22
  12.6 7.2 %all-to-all-start.2 = ((bf16[16,256,256]{1,2,0:T(8,128)(2,1)}), bf16[16,256,256]{1,2,0:T(8,128)(2,1)}, u32[]{:S(2)}, u32[]{:S(2)}) async-start(bf16[16,256,256]{1,2,0:T(8,128)(2,1)} %stack.22), calls=%async_computation.3 | async-start | bytes 4194304 | tf_op jit(solution)/shard_map/all_to_all | solution.py:122
  24.2 25.9 %all-to-all-done.2 = bf16[16,256,256]{1,2,0:T(8,128)(2,1)} async-done(((bf16[16,256,256]{1,2,0:T(8,128)(2,1)}), bf16[16,256,256]{1,2,0:T(8,128)(2,1)}, u32[]{:S(2)}, u32[]{:S(2)}) %all-to-all-start.2) | async-done | bytes 2097184 | tf_op jit(solution)/shard_map/all_to_all | solution.py:122
  50.1 2.3 fusion.74
  54.0 16.2 %all-to-all-start.3 = ((bf16[32,8,256]{2,1,0:T(8,128)(2,1)}), bf16[32,8,256]{2,1,0:T(8,128)(2,1)S(1)}, u32[]{:S(2)}, u32[]{:S(2)}) async-start(bf16[32,8,256]{2,1,0:T(8,128)(2,1)} %bitcast.23), calls=%async_computation.4 | async-start | bytes 262144 | tf_op jit(solution)/shard_map/all_to_all | solution.py:88
  70.6 3.4 fusion.73
  74.0 11.8 %all-to-all-done.3 = bf16[32,8,256]{2,1,0:T(8,128)(2,1)S(1)} async-done(((bf16[32,8,256]{2,1,0:T(8,128)(2,1)}), bf16[32,8,256]{2,1,0:T(8,128)(2,1)S(1)}, u32[]{:S(2)}, u32[]{:S(2)}) %all-to-all-start.3) | async-done | bytes 131104 | tf_op jit(solution)/shard_map/all_to_all | solution.py:88
  85.9 21.2 %rev.7 = f32[8,8192]{1,0:T(8,128)} reverse(f32[8,8192]{1,0:T(8,128)S(1)} %bitcast.140), dimensions={1} | reverse | bytes 524288 | tf_op jit(solution)/shard_map/jit(_flip)/rev | solution.py:89
  109.2 1.8 slice.453
  112.1 1.8 slice.423
  122.3 1.6 multiply_add_fusion.3
  123.9 1.6 slice.447
  125.5 1.7 slice.433
  127.2 1.6 slice.432
  128.8 1.6 multiply_add_fusion.2
  130.4 1.6 slice.445
  132.0 1.6 slice.436
  133.6 1.6 slice.435
  137.5 2.7 fusion.17
  146.7 3.2 pad.107
  152.3 3.2 pad.109
  162.4 1.6 pad.161
  164.0 1.6 pad.217
  165.6 2.1 convolution_add_fusion
  169.8 23.9 %rev.8 = f32[8,8192]{1,0:T(8,128)S(1)} reverse(f32[8,8192]{1,0:T(8,128)} %reshape.79), dimensions={1} | reverse | bytes 524288 | tf_op jit(solution)/shard_map/jit(_flip)/rev | solution.py:90
  193.7 26.1 %all_to_all.72 = f32[8,32,256]{2,0,1:T(8,128)} all-to-all(f32[8,32,256]{2,0,1:T(8,128)S(1)} %bitcast.141), channel_id=1, replica_groups=mesh['ctx'=32,'ch'=16] {'ctx'}, dimensions={1} | all-to-all | bytes 524288 | tf_op jit(solution)/shard_map/all_to_all | solution.py:93
  222.7 20.7 %all_to_all.73 = bf16[32,8,256]{2,1,0:T(8,128)(2,1)S(1)} all-to-all(bf16[32,8,256]{2,1,0:T(8,128)(2,1)S(1)} %bitcast.150), channel_id=1, replica_groups=mesh['ctx'=32,'ch'=16] {'ctx'}, dimensions={0} | all-to-all | bytes 262144 | tf_op jit(solution)/shard_map/all_to_all | solution.py:79
  247.7 1.8 slice.420
  261.1 1.6 fusion.71
  263.3 3.1 pad.91
  270.3 4.9 %pad.92 = f32[8,8,16]{1,2,0:T(8,128)} pad(f32[8,4,16]{1,2,0:T(8,128)} %pad_maximum_fusion.1, f32[]{:T(128)} %constant.7.clone.1), padding=0_0_0x0_1_1x0_0_0 | pad | bytes 6148 | tf_op jit(solution)/shard_map/pad | solution.py:53
  275.2 4.9 %pad.93 = f32[8,8,16]{1,2,0:T(8,128)} pad(f32[8,4,16]{1,2,0:T(8,128)} %add.260, f32[]{:T(128)} %constant.7.clone.1), padding=0_0_0x1_0_1x0_0_0 | pad | bytes 6148 | tf_op jit(solution)/shard_map/pad | solution.py:53
  280.1 1.5 add.262
  283.3 3.2 pad.94
  286.6 5.0 %pad.95 = f32[8,16,16]{1,2,0:T(8,128)} pad(f32[8,8,16]{1,2,0:T(8,128)} %add.262, f32[]{:T(128)} %constant.7.clone.1), padding=0_0_0x1_0_1x0_0_0 | pad | bytes 12292 | tf_op jit(solution)/shard_map/pad | solution.py:53
  291.5 1.5 add.264
  294.8 3.3 pad.97
  300.8 3.5 pad.99
  305.3 1.6 pad.159
  306.9 1.6 pad.216
  308.6 2.1 convolution_add_fusion.1
  313.8 25.2 %all_to_all.74 = f32[8,32,256]{2,0,1:T(8,128)S(1)} all-to-all(f32[8,32,256]{2,0,1:T(8,128)S(1)} %copy.87), channel_id=1, replica_groups=mesh['ctx'=32,'ch'=16] {'ctx'}, dimensions={1} | all-to-all | bytes 524288 | tf_op jit(solution)/shard_map/all_to_all | solution.py:84
  339.2 2.7 fusion.24
  342.9 2.5 collective-permute-start.1
  345.5 1.4 collective-permute-done.1
  348.4 80.3 %reduce-scatter.2.cloned.1.call-done = f32[256,256]{1,0:T(8,128)} async-done(((f32[256,4096]{1,0:T(8,128)}), f32[256,256]{1,0:T(8,128)}) %reduce-scatter.2.cloned.1.call-update) | async-done | bytes 262160 | tf_op jit(solution)/shard_map/reduce_scatter | solution.py:116
  428.7 1.6 convert_element_type.43
  (202 shorter events, 75.8 us)
Async XLA Ops:
  7.2 42.9 %copy-start = (bf16[256,4096]{1,0:T(8,128)(2,1)S(1)}, bf16[256,4096]{1,0:T(8,128)(2,1)}, u32[]{:S(2)}) copy-start(bf16[256,4096]{1,0:T(8,128)(2,1)} %param.15) | copy-start | bytes 6291460
  8.1 15.3 %collective-permute-start = (bf16[3,6,256]{2,1,0:T(8,128)(2,1)S(1)}, bf16[3,6,256]{2,1,0:T(8,128)(2,1)S(1)}, u32[]{:S(2)}, u32[]{:S(2)}) collective-permute-start(bf16[3,6,256]{2,1,0:T(8,128)(2,1)S(1)} %pad_maximum_fusion.14), channel_id=1, source_target_pairs={{0,16},{16,32},{32,48},{48,64},{64,80},{80,96},{96,112},{112,128},... | collective-permute-start | bytes 27656 | tf_op jit(solution)/shard_map/ppermute | solution.py:14
  12.5 7.3 %copy-start.34 = (f32[256,16]{0,1:T(8,128)S(1)}, f32[256,16]{0,1:T(8,128)}, u32[]{:S(2)}) copy-start(f32[256,16]{0,1:T(8,128)} %param.14) | copy-start | bytes 49156
  12.5 7.3 %copy-start.35 = (f32[256,16]{0,1:T(8,128)S(1)}, f32[256,16]{0,1:T(8,128)}, u32[]{:S(2)}) copy-start(f32[256,16]{0,1:T(8,128)} %param.13) | copy-start | bytes 49156
  12.6 8.1 %copy-start.33 = (f32[7,3,256]{2,0,1:T(8,128)S(1)}, f32[7,3,256]{2,0,1:T(8,128)}, u32[]{:S(2)}) copy-start(f32[7,3,256]{2,0,1:T(8,128)} %param.12) | copy-start | bytes 64516
  12.6 10.9 %copy-start.13 = (bf16[256,256]{1,0:T(8,128)(2,1)S(1)}, bf16[256,256]{1,0:T(8,128)(2,1)}, u32[]{:S(2)}) copy-start(bf16[256,256]{1,0:T(8,128)(2,1)} %param.11) | copy-start | bytes 393220
  12.6 10.9 %copy-start.14 = (bf16[256,256]{1,0:T(8,128)(2,1)S(1)}, bf16[256,256]{1,0:T(8,128)(2,1)}, u32[]{:S(2)}) copy-start(bf16[256,256]{1,0:T(8,128)(2,1)} %param.10) | copy-start | bytes 393220
  12.6 10.8 %copy-start.15 = (bf16[256,256]{1,0:T(8,128)(2,1)S(1)}, bf16[256,256]{1,0:T(8,128)(2,1)}, u32[]{:S(2)}) copy-start(bf16[256,256]{1,0:T(8,128)(2,1)} %param.9) | copy-start | bytes 393220
  12.6 37.5 %all-to-all-start.2 = ((bf16[16,256,256]{1,2,0:T(8,128)(2,1)}), bf16[16,256,256]{1,2,0:T(8,128)(2,1)}, u32[]{:S(2)}, u32[]{:S(2)}) async-start(bf16[16,256,256]{1,2,0:T(8,128)(2,1)} %stack.22), calls=%async_computation.3 | async-start | bytes 4194304 | tf_op jit(solution)/shard_map/all_to_all | solution.py:122
  20.1 88.1 %copy-start.36 = (f32[64]{0:T(128)}, f32[64]{0:T(128)S(1)}, u32[]{:S(2)}) copy-start(f32[64]{0:T(128)S(1)} %iota_subtract_fusion) | copy-start | bytes 772
  20.7 3.5 copy-start.19
  20.7 3.5 copy-start.21
  20.7 3.5 copy-start.23
  20.7 3.5 copy-start.25
  20.8 3.4 copy-start.27
  20.8 3.4 copy-start.29
  21.4 49.0 %copy-start.17 = (f32[8,16]{1,0:T(8,128)}, f32[8,16]{1,0:T(8,128)S(1)}, u32[]{:S(2)}) copy-start(f32[8,16]{1,0:T(8,128)S(1)} %get-tuple-element.34) | copy-start | bytes 1540
  21.9 2.3 copy-start.31
  52.5 0.7 copy-start.1
  54.0 31.9 %all-to-all-start.3 = ((bf16[32,8,256]{2,1,0:T(8,128)(2,1)}), bf16[32,8,256]{2,1,0:T(8,128)(2,1)S(1)}, u32[]{:S(2)}, u32[]{:S(2)}) async-start(bf16[32,8,256]{2,1,0:T(8,128)(2,1)} %bitcast.23), calls=%async_computation.4 | async-start | bytes 262144 | tf_op jit(solution)/shard_map/all_to_all | solution.py:88
  70.1 358.5 %reduce-scatter.2.cloned.1.call-start = ((), (), s32[]{:S(2)}) async-start(), calls=%async_computation.6 | async-start | bytes 4456448 | tf_op jit(solution)/shard_map/reduce_scatter | solution.py:116
  109.2 4.7 %copy-start.8 = (f32[8,128,16]{1,2,0:T(8,128)}, f32[8,128,16]{1,2,0:T(8,128)S(1)}, u32[]{:S(2)}) copy-start(f32[8,128,16]{1,2,0:T(8,128)S(1)} %fusion.42) | copy-start | bytes 196612
  119.4 15.7 %copy-start.4 = (f32[8,32,16]{1,2,0:T(8,128)}, f32[8,32,16]{1,2,0:T(8,128)S(1)}, u32[]{:S(2)}) copy-start(f32[8,32,16]{1,2,0:T(8,128)S(1)} %multiply_add_fusion.4) | copy-start | bytes 49156
  140.3 5.8 %copy-start.7 = (f32[8,8,16]{1,2,0:T(8,128)S(1)}, f32[8,8,16]{1,2,0:T(8,128)}, u32[]{:S(2)}) copy-start(f32[8,8,16]{1,2,0:T(8,128)} %multiply_add_fusion.2) | copy-start | bytes 12292
  140.3 11.2 %copy-start.6 = (f32[8,16,16]{1,2,0:T(8,128)S(1)}, f32[8,16,16]{1,2,0:T(8,128)}, u32[]{:S(2)}) copy-start(f32[8,16,16]{1,2,0:T(8,128)} %multiply_add_fusion.3) | copy-start | bytes 24580
  140.3 16.2 %copy-start.5 = (f32[8,32,16]{1,2,0:T(8,128)S(1)}, f32[8,32,16]{1,2,0:T(8,128)}, u32[]{:S(2)}) copy-start(f32[8,32,16]{1,2,0:T(8,128)} %copy-done.4) | copy-start | bytes 49156
  144.5 17.8 %copy-start.9 = (f32[8,128,16]{1,2,0:T(8,128)S(1)}, f32[8,128,16]{1,2,0:T(8,128)}, u32[]{:S(2)}) copy-start(f32[8,128,16]{1,2,0:T(8,128)} %copy-done.8) | copy-start | bytes 196612
  146.1 19.5 %copy-start.12 = (f32[8,128,64]{1,2,0:T(8,128)S(1)}, f32[8,128,64]{1,2,0:T(8,128)}, u32[]{:S(2)}) copy-start(f32[8,128,64]{1,2,0:T(8,128)} %fusion.17) | copy-start | bytes 786436
  169.8 75.4 %copy-start.3 = (f32[8,64,64]{2,0,1:T(8,128)S(1)}, f32[8,64,64]{2,0,1:T(8,128)}, u32[]{:S(2)}) copy-start(f32[8,64,64]{2,0,1:T(8,128)} %fusion.73) | copy-start | bytes 393220
  247.7 9.6 %copy-start.16 = (f32[8,16]{1,0:T(8,128)S(1)}, f32[8,16]{1,0:T(8,128)}, u32[]{:S(2)}) copy-start(f32[8,16]{1,0:T(8,128)} %get-tuple-element.30) | copy-start | bytes 1540
  270.3 38.3 %copy-start.11 = (f32[8,128,64]{1,2,0:T(8,128)S(1)}, f32[8,128,64]{1,2,0:T(8,128)}, u32[]{:S(2)}) copy-start(f32[8,128,64]{1,2,0:T(8,128)} %fusion.19) | copy-start | bytes 786436
  293.9 14.7 %copy-start.18 = (f32[8,16]{1,0:T(8,128)S(1)}, f32[8,16]{1,0:T(8,128)}, u32[]{:S(2)}) copy-start(f32[8,16]{1,0:T(8,128)} %copy-done.17) | copy-start | bytes 1540
  341.9 0.9 copy-start.2
  341.9 1.0 copy-start.10
  342.8 4.1 copy-start.20
  342.8 4.1 copy-start.22
  342.8 4.1 copy-start.24
  342.8 4.1 copy-start.26
  342.8 4.1 copy-start.28
  342.8 4.1 copy-start.30
  342.8 4.1 copy-start.32
  342.9 3.9 collective-permute-start.1
Sparse Core Ops, SparseCore 0:
  342.0 86.6 reduce-scatter.1
